TPU v7x, 256 devices: a whole 4x4x8 slice. The times are simulated.
256 devices in a mesh: tok: 16 (over y, x), ch: 16 (over z, core).
Axes of the slice: x: 4, y: 4, z: 8, core: 2. Of those that a mesh axis runs over, the one named last changes fastest.
Arguments:
- tokens: bfloat16 [256, 16384], P('tok', 'ch'), may hold values from -64 to 64
- probe: int32 [256, 16384], P('tok', 'ch'), may hold values from 0 to 1
- signs: int32 [16384], P('ch'), may hold values from 0 to 1
- gate_weight: bfloat16 [16384, 26624], P('ch', 'tok'), may hold values from -0.046875 to 0.046875
- up_weight: bfloat16 [16384, 26624], P('ch', 'tok'), may hold values from -0.046875 to 0.046875
- down_weight: bfloat16 [26624, 16384], P('tok', 'ch'), may hold values from -0.0390625 to 0.0390625
Outputs:
- rotated_product: float32 [256, 16384], P('tok', 'ch')
- diagonal_estimate: float32 [16384], P('ch')
All inputs are finite; a program needn't handle non-finite values.
Results may differ from a plain program's by a relative error of at most 0.004.
Values may be sent and summed in bfloat16 or wider, within the bound.
No kernel may reach another device: no remote copies, remote signals or barrier semaphores. Data moves between devices by JAX's collectives and lax.ppermute only.
A program may use at most 128 MiB of HBM per device.

v0:
```python
import math
import jax
import jax.numpy as jnp
from jax import lax
from jax.sharding import PartitionSpec as P

D = 16384


def partner_2(value, axis, stride):
    mask = 2**stride
    pairs = [(source, source ^ mask) for source in range(lax.axis_size(axis))]
    return lax.ppermute(value, axis, pairs)


def sign_table(length):
    indices = jnp.arange(length, dtype=jnp.int32)
    parity = jnp.zeros((length, length), jnp.int32)
    for bit_pos in range(length.bit_length() - 1):
        parity = parity + (indices[:, None] >> bit_pos & 1) * (indices[None, :] >> bit_pos & 1)
    return jnp.where(parity % 2 == 0, 1.0, -1.0).astype(jnp.float32)


def cross_pairs(values):
    my_index = lax.axis_index("ch")
    for bit_pos in range(lax.axis_size("ch").bit_length() - 1):
        partner = partner_2(values, "ch", bit_pos)
        upper_half = my_index >> bit_pos & 1 == 1
        values = jnp.where(upper_half, partner - values, values + partner)
    return values


def cross_section(values):
    return cross_pairs(values)


def grad_product(gate_piece, up_piece, gate_weight, up_weight):
    contract = (((1,), (1,)), ((), ()))
    first_term = lax.dot_general(
        gate_piece, gate_weight, contract, preferred_element_type=jnp.float32
    )
    return first_term + lax.dot_general(
        up_piece, up_weight, contract, preferred_element_type=jnp.float32
    )


def on_device(tokens, probe, signs, gate_weight, up_weight, down_weight):
    tok_rows, channels = tokens.shape
    total_rows = tok_rows * lax.axis_size("tok")
    root_scale = 1.0 / math.sqrt(D)
    hadamard = sign_table(channels)
    probe_signs = (2 * probe - 1).astype(jnp.float32)
    channel_signs = (2 * signs - 1).astype(jnp.float32)
    start_local = jnp.dot(
        (probe_signs * channel_signs[None, :]).astype(jnp.bfloat16),
        hadamard.astype(jnp.bfloat16),
        preferred_element_type=jnp.float32,
    )
    tangent = (cross_section(start_local) * root_scale).astype(jnp.bfloat16)
    all_tokens, all_tangent = (
        lax.all_gather(tokens, "tok", axis=0, tiled=True),
        lax.all_gather(tangent, "tok", axis=0, tiled=True),
    )
    inputs = jnp.stack([all_tokens, all_tangent], axis=1)
    gate_part = jnp.einsum("rsd,df->rsf", inputs, gate_weight, preferred_element_type=jnp.float32)
    up_part = jnp.einsum("rsd,df->rsf", inputs, up_weight, preferred_element_type=jnp.float32)
    summed = lax.psum_scatter(
        jnp.stack([gate_part, up_part], axis=2), "ch", scatter_dimension=0, tiled=True
    )
    gate_pre = summed[:, 0, 0]
    up_pre = summed[:, 0, 1]
    gate_tan = summed[:, 1, 0]
    up_tan = summed[:, 1, 1]
    sigmoid_gate = jax.nn.sigmoid(gate_pre)
    activated = gate_pre * sigmoid_gate
    slope_term = sigmoid_gate * (1.0 + gate_pre * (1.0 - sigmoid_gate))
    hidden_tan = (slope_term * gate_tan * up_pre + activated * up_tan).astype(jnp.bfloat16)
    out_part = jnp.dot(
        lax.all_gather(hidden_tan, "ch", axis=0, tiled=True),
        down_weight,
        preferred_element_type=jnp.float32,
    )
    out_tangent = lax.psum(out_part, "tok").astype(jnp.bfloat16)
    piece = out_tangent
    back_hidden = lax.psum_scatter(
        lax.dot_general(
            piece, down_weight, (((1,), (1,)), ((), ())), preferred_element_type=jnp.float32
        ),
        "ch",
        scatter_dimension=0,
        tiled=True,
    )
    back_gate = (back_hidden * up_pre * slope_term).astype(jnp.bfloat16)
    back_up = (back_hidden * activated).astype(jnp.bfloat16)
    stacked = jnp.stack([back_gate, back_up], axis=1)
    piece = lax.all_gather(stacked, "ch", axis=0, tiled=True)
    in_part = grad_product(piece[:, 0], piece[:, 1], gate_weight, up_weight)
    back_tokens = lax.psum_scatter(in_part, "tok", scatter_dimension=0, tiled=True)
    local_back = jnp.dot(
        back_tokens, hadamard, precision=lax.Precision.HIGHEST, preferred_element_type=jnp.float32
    )
    rotated_product = cross_section(local_back) * root_scale * channel_signs[None, :]
    token_terms = jnp.sum(probe_signs * rotated_product, axis=0)
    diagonal_estimate = lax.psum(token_terms, "tok") / total_rows
    return (rotated_product, diagonal_estimate)


def solution(mesh):
    placed = (
        P("tok", "ch"),
        P("tok", "ch"),
        P("ch"),
        P("ch", "tok"),
        P("ch", "tok"),
        P("tok", "ch"),
    )
    return jax.shard_map(
        on_device, mesh=mesh, in_specs=placed, out_specs=(P("tok", "ch"), P("ch")), check_vma=False
    )
```

profile of v0, /device:TPU:32, one launch (start us, length us, event | category | flops | bytes accessed | tf_op | source)
XLA Modules:
  0.0 515.5 jit_solution(10228923519675699118)
XLA Ops:
  7.2 0.0 copy-start
  7.2 0.0 reduce-scatter.4.cloned.1.call-start
  7.3 0.8 add_convert_fusion
  8.1 6.5 %fusion.3 = pred[1024,1024]{1,0:T(32,128)(4,1)S(1)} fusion(s32[1024]{0:T(1024)S(1)} %get-tuple-element.6, s32[1024]{0:T(1024)S(1)} %get-tuple-element.7, s32[1024]{0:T(1024)S(1)} %get-tuple-element.8, s32[1024]{0:T(1024)S(1)} %get-tuple-element.9, s32[1024]{0:T(1024)S(1)} %get-tuple-element.10, s32[1024]{0:T(1024)S(1)} %get-tuple-element.11, ...), kind=kLoop, calls=%fused_computation.8 | loop fusion | flops 32505856 | bytes 1089536 | tf_op jit(solution)/shard_map/eq | solution.py:21
  14.6 0.0 copy-start.1
  14.6 1.0 copy-done.1
  15.6 1.4 fusion.14
  17.0 0.0 collective-permute-start
  17.0 1.4 collective-permute-done
  18.4 0.8 add_select_fusion.6
  19.2 1.9 collective-permute-start.1
  21.2 2.5 collective-permute-done.1
  23.7 0.8 add_select_fusion.5
  24.5 3.4 collective-permute-start.2
  27.9 2.3 collective-permute-done.2
  30.2 6.1 %collective-permute-start.3 = (f32[16,1024]{1,0:T(8,128)S(1)}, f32[16,1024]{1,0:T(8,128)S(1)}, u32[]{:S(2)}, u32[]{:S(2)}) collective-permute-start(f32[16,1024]{1,0:T(8,128)S(1)} %add_select_fusion.4), channel_id=1, source_target_pairs={{0,8},{1,9},{2,10},{3,11},{4,12},{5,13},{6,14},{7,15},{8,0},{9,1},... | collective-permute-start | bytes 196616 | tf_op jit(solution)/shard_map/ppermute | solution.py:13
  36.3 24.4 %all_gather.12 = bf16[256,1024]{1,0:T(8,128)(2,1)S(1)} all-gather(bf16[16,1024]{1,0:T(8,128)(2,1)} %param.6), channel_id=1, replica_groups=mesh['tok'=16,'ch'=16] {'tok'}, dimensions={0}, use_global_device_ids=true | all-gather | bytes 557056 | tf_op jit(solution)/shard_map/all_gather | solution.py:61
  60.6 0.0 collective-permute-done.3
  60.7 23.3 %all_gather.13 = bf16[256,1024]{1,0:T(8,128)(2,1)S(1)} all-gather(bf16[16,1024]{1,0:T(8,128)(2,1)S(1)} %multiply_convert_fusion.2), channel_id=1, replica_groups=mesh['tok'=16,'ch'=16] {'tok'}, dimensions={0}, use_global_device_ids=true | all-gather | bytes 557056 | tf_op jit(solution)/shard_map/all_gather | solution.py:62
  84.0 4.0 fusion.11
  88.0 0.0 copy-done
  88.0 2.1 fusion.8
  90.1 3.3 pad_maximum_fusion
  93.4 0.0 reduce-scatter.4.cloned.1.call-update
  93.4 0.0 reduce-scatter.6.cloned.1.call-start
  93.4 60.3 %reduce-scatter.4.cloned.1.call-done = f32[16,2,2,1664]{3,0,1,2:T(8,128)} async-done(((f32[256,2,2,1664]{3,0,1,2:T(8,128)}), f32[16,2,2,1664]{3,0,1,2:T(8,128)}) %reduce-scatter.4.cloned.1.call-update) | async-done | bytes 426000 | tf_op jit(solution)/shard_map/reduce_scatter | solution.py:67
  153.7 1.1 fusion.24
  154.8 20.4 %all_gather.14 = bf16[256,1664]{1,0:T(8,128)(2,1)S(1)} all-gather(bf16[16,1664]{1,0:T(8,128)(2,1)S(1)} %fusion.24), channel_id=1, replica_groups=mesh['tok'=16,'ch'=16] {'ch'}, dimensions={0}, use_global_device_ids=true | all-gather | bytes 905216 | tf_op jit(solution)/shard_map/all_gather | solution.py:79
  175.3 4.1 fusion.41
  179.4 88.3 %all-reduce.1 = bf16[256,1024]{1,0:T(8,128)(2,1)} all-reduce(f32[256,1024]{1,0:T(8,128)} %fusion.41), channel_id=1, replica_groups=mesh['tok'=16,'ch'=16] {'tok'}, use_global_device_ids=true, to_apply=%region_1.2 | all-reduce | flops 262144 | bytes 1572864 | tf_op jit(solution)/shard_map/psum | solution.py:83
  267.7 4.5 fusion.42
  272.2 0.0 reduce-scatter.6.cloned.1.call-update
  272.2 0.0 all-gather.2.cloned.1.call-start
  272.3 49.8 %reduce-scatter.6.cloned.1.call-done = f32[16,1664]{1,0:T(8,128)} async-done(((f32[256,1664]{1,0:T(8,128)}), f32[16,1664]{1,0:T(8,128)}) %reduce-scatter.6.cloned.1.call-update) | async-done | bytes 106512 | tf_op jit(solution)/shard_map/reduce_scatter | solution.py:85
  322.1 1.1 fusion.28
  323.1 0.7 pad_maximum_fusion.4
  323.8 0.0 all-gather.2.cloned.1.call-update
  323.8 0.2 reduce-scatter.8.cloned.1.call-start
  324.1 40.5 %all-gather.2.cloned.1.call-done = bf16[256,2,1664]{2,0,1:T(8,128)(2,1)} async-done(((bf16[16,2,1664]{2,0,1:T(8,128)(2,1)}), bf16[256,2,1664]{2,0,1:T(8,128)(2,1)}) %all-gather.2.cloned.1.call-update) | async-done | bytes 1703952 | tf_op jit(solution)/shard_map/all_gather | solution.py:96
  364.6 0.0 copy-start.4
  364.6 0.0 copy-start.5
  364.6 2.4 fusion.19
  367.0 0.0 copy-done.4
  367.0 0.3 copy-done.5
  367.3 0.0 copy-start.3
  367.3 0.0 copy-start.2
  367.3 2.1 convolution_add_fusion
  369.5 0.0 reduce-scatter.8.cloned.1.call-update
  369.5 77.1 %reduce-scatter.8.cloned.1.call-done = f32[16,1024]{1,0:T(8,128)} async-done(((f32[256,1024]{1,0:T(8,128)}), f32[16,1024]{1,0:T(8,128)}) %reduce-scatter.8.cloned.1.call-update) | async-done | bytes 65552 | tf_op jit(solution)/shard_map/reduce_scatter | solution.py:98
  446.6 3.6 fusion
  450.2 0.0 collective-permute-start.4
  450.2 1.2 collective-permute-done.4
  451.4 0.5 collective-permute-start.5
  452.0 3.8 collective-permute-done.5
  455.8 2.6 collective-permute-start.6
  458.4 2.6 collective-permute-done.6
  461.1 5.0 collective-permute-start.7
  466.1 0.0 copy-done.3
  466.1 3.5 collective-permute-done.7
  469.6 0.0 copy-done.2
  469.6 0.7 multiply_reduce_fusion
  470.3 38.1 %psum.15 = f32[1024]{0:T(1024)S(1)} all-reduce(f32[1024]{0:T(1024)S(1)} %get-tuple-element.2), channel_id=1, replica_groups=mesh['tok'=16,'ch'=16] {'tok'}, use_global_device_ids=true, to_apply=%region_5.6 | all-reduce | flops 1024 | bytes 8192 | tf_op jit(solution)/shard_map/psum | solution.py:104
  508.4 0.6 broadcast_multiply_fusion
  (11 shorter events, 0.1 us)
Async XLA Ops:
  7.2 80.8 %copy-start = (bf16[1024,1664]{1,0:T(8,128)(2,1)S(1)}, bf16[1024,1664]{1,0:T(8,128)(2,1)}, u32[]{:S(2)}) copy-start(bf16[1024,1664]{1,0:T(8,128)(2,1)} %param.9) | copy-start | bytes 10223620
  7.2 146.5 %reduce-scatter.4.cloned.1.call-start = ((), (), s32[]{:S(2)}) async-start(), calls=%async_computation.3 | async-start | bytes 7241728 | tf_op jit(solution)/shard_map/reduce_scatter | solution.py:67
  14.6 1.0 copy-start.1
  17.0 1.4 collective-permute-start
  19.2 4.5 collective-permute-start.1
  24.5 5.7 %collective-permute-start.2 = (f32[16,1024]{1,0:T(8,128)S(1)}, f32[16,1024]{1,0:T(8,128)S(1)}, u32[]{:S(2)}, u32[]{:S(2)}) collective-permute-start(f32[16,1024]{1,0:T(8,128)S(1)} %add_select_fusion.5), channel_id=1, source_target_pairs={{0,4},{1,5},{2,6},{3,7},{4,0},{5,1},{6,2},{7,3},{8,12},{9,13},{10,... | collective-permute-start | bytes 196616 | tf_op jit(solution)/shard_map/ppermute | solution.py:13
  30.2 30.4 %collective-permute-start.3 = (f32[16,1024]{1,0:T(8,128)S(1)}, f32[16,1024]{1,0:T(8,128)S(1)}, u32[]{:S(2)}, u32[]{:S(2)}) collective-permute-start(f32[16,1024]{1,0:T(8,128)S(1)} %add_select_fusion.4), channel_id=1, source_target_pairs={{0,8},{1,9},{2,10},{3,11},{4,12},{5,13},{6,14},{7,15},{8,0},{9,1},... | collective-permute-start | bytes 196616 | tf_op jit(solution)/shard_map/ppermute | solution.py:13
  93.4 228.7 %reduce-scatter.6.cloned.1.call-start = ((), (), s32[]{:S(2)}) async-start(), calls=%async_computation.4 | async-start | bytes 1810432 | tf_op jit(solution)/shard_map/reduce_scatter | solution.py:85
  272.2 92.4 %all-gather.2.cloned.1.call-start = ((), (), s32[]{:S(2)}) async-start(), calls=%async_computation.5 | async-start | bytes 1810432 | tf_op jit(solution)/shard_map/all_gather | solution.py:96
  323.8 122.8 %reduce-scatter.8.cloned.1.call-start = ((), (), s32[]{:S(2)}) async-start(), calls=%async_computation.6 | async-start | bytes 1114112 | tf_op jit(solution)/shard_map/reduce_scatter | solution.py:98
  364.6 2.5 copy-start.4
  364.6 2.7 copy-start.5
  367.3 98.8 %copy-start.3 = (s32[1024]{0:T(1024)S(1)}, s32[1024]{0:T(1024)}, u32[]{:S(2)}) copy-start(s32[1024]{0:T(1024)} %param.8) | copy-start | bytes 12292
  367.3 102.3 %copy-start.2 = (s32[16,1024]{1,0:T(8,128)S(1)}, s32[16,1024]{1,0:T(8,128)}, u32[]{:S(2)}) copy-start(s32[16,1024]{1,0:T(8,128)} %param.7) | copy-start | bytes 196612
  450.2 1.3 collective-permute-start.4
  451.4 4.4 collective-permute-start.5
  455.8 5.3 %collective-permute-start.6 = (f32[16,1024]{1,0:T(8,128)S(1)}, f32[16,1024]{1,0:T(8,128)S(1)}, u32[]{:S(2)}, u32[]{:S(2)}) collective-permute-start(f32[16,1024]{1,0:T(8,128)S(1)} %add_select_fusion.2), channel_id=1, source_target_pairs={{0,4},{1,5},{2,6},{3,7},{4,0},{5,1},{6,2},{7,3},{8,12},{9,13},{10,... | collective-permute-start | bytes 196616 | tf_op jit(solution)/shard_map/ppermute | solution.py:13
  461.1 8.5 %collective-permute-start.7 = (f32[16,1024]{1,0:T(8,128)S(1)}, f32[16,1024]{1,0:T(8,128)S(1)}, u32[]{:S(2)}, u32[]{:S(2)}) collective-permute-start(f32[16,1024]{1,0:T(8,128)S(1)} %add_select_fusion.1), channel_id=1, source_target_pairs={{0,8},{1,9},{2,10},{3,11},{4,12},{5,13},{6,14},{7,15},{8,0},{9,1},... | collective-permute-start | bytes 196616 | tf_op jit(solution)/shard_map/ppermute | solution.py:13
Sparse Core Ops, SparseCore 0:
  93.5 60.1 reduce-scatter.3
  272.3 49.7 reduce-scatter.5
  324.1 40.4 all-gather.1
  369.6 76.9 reduce-scatter.7
where the time goes:
time: 516 us
  waiting for transfers between devices  245 us (47%)
  blocking collectives  195 us (38%)
  matrix products  24.3 us (5%)
  starting transfers between devices  19.8 us (4%)
  other arithmetic  16.4 us (3%)
  between operations  13.9 us (3%)
    psum x1, blocking collectives, on_device(): out_tangent = lax.psum(out_part, 'tok').astype(jnp.bfloat16)  88.3 us
    reduce_scatter x1, waiting for transfers between devices, on_device(): lax.psum_scatter(in_part, 'tok', scatter_dimension=0, tiled=True)  77.1 us
    reduce_scatter x1, waiting for transfers between devices, on_device(): lax.psum_scatter(jnp.stack([gate_part, up_part], axis=2), 'ch', scatter_d...  60.3 us
    reduce_scatter x1, waiting for transfers between devices, on_device(): lax.psum_scatter(lax.dot_general(piece, down_weight, (((1,), (1,)), ((),...  49.8 us
    all_gather x1, waiting for transfers between devices, on_device(): piece = lax.all_gather(stacked, 'ch', axis=0, tiled=True)  40.5 us
    psum x1, blocking collectives, on_device(): diagonal_estimate = lax.psum(token_terms, 'tok') / total_rows  38.1 us
    all_gather x1, blocking collectives, on_device(): lax.all_gather(tokens, 'tok', axis=0, tiled=True)  24.4 us
    all_gather x1, blocking collectives, on_device(): lax.all_gather(tangent, 'tok', axis=0, tiled=True)  23.3 us
  transfers between devices with their start and end apart: 12, of which 11 were waited for; matrix products, arithmetic and copies ran while one was open for 0% of the time, Pallas kernels for 0%

commit v1 on v0

--- a/solution.py
+++ b/solution.py
@@ -5,6 +5,12 @@
 from jax.sharding import PartitionSpec as P
 
 D = 16384
+
+
+def _try_all_positions(here_x, d_out):
+    right_arr = list(here_x.shape[1:])
+    right_arr[d_out] *= here_x.shape[0]
+    return jnp.moveaxis(here_x, 0, d_out).reshape(right_arr)
 
 
 def partner_2(value, axis, stride):
@@ -93,7 +99,31 @@
     back_gate = (back_hidden * up_pre * slope_term).astype(jnp.bfloat16)
     back_up = (back_hidden * activated).astype(jnp.bfloat16)
     stacked = jnp.stack([back_gate, back_up], axis=1)
-    piece = lax.all_gather(stacked, "ch", axis=0, tiled=True)
+    buffers = []
+    c = 0
+    axis_total = lax.axis_size("ch")
+    while c < axis_total:
+        buffers.append((c, (c + 1) % axis_total))
+        c += 1
+    kept_rows = []
+    for k0, num in buffers:
+        kept_rows.append((num, k0))
+    t = 0
+    local_out, block_last = ([], [])
+    while t < axis_total - 1:
+        if t % 2 == 0:
+            p_next = lax.ppermute(local_out[-1] if local_out else stacked, "ch", buffers)
+            local_out.append(p_next)
+        else:
+            front = lax.ppermute(block_last[-1] if block_last else stacked, "ch", kept_rows)
+            block_last.append(front)
+        t += 1
+    arr_out = jnp.stack([*local_out[::-1], stacked, *block_last], axis=0)
+    part_now = len(local_out)
+    passed = lax.axis_index("ch")
+    tile_out = passed - part_now
+    arr_out = arr_out[(jnp.arange(axis_total) - tile_out) % axis_total]
+    piece = _try_all_positions(arr_out, 0)
     in_part = grad_product(piece[:, 0], piece[:, 1], gate_weight, up_weight)
     back_tokens = lax.psum_scatter(in_part, "tok", scatter_dimension=0, tiled=True)
     local_back = jnp.dot(

time: 516 us -> 545 us (1.056)
  local copies, waits for them, and re-layouts: 1.26 us -> 26.7 us
  starting transfers between devices: 19.8 us -> 38.6 us
  waiting for transfers between devices: 245 us -> 231 us
    all_gather x1 -> x0, waiting for transfers between devices: 40.5 us -> none  [on_device(): piece = lax.all_gather(stacked, 'ch', axis=0, tiled=True)]
    ppermute x0 -> x15, waiting for transfers between devices: none -> 20.1 us  [the longest x8 16.6 us: on_device(): lax.ppermute(local_out[-1] if local_out else stacked, 'ch', buffers)]
    unnamed x12 -> x36, local copies, waits for them, and re-layouts: 1.26 us -> 21.1 us
    ppermute x0 -> x15, starting transfers between devices: none -> 18.8 us  [the longest x7 18.7 us: on_device(): lax.ppermute(block_last[-1] if block_last else stacked, 'ch', kept_rows)]
    reduce_scatter x1, waiting for transfers between devices: 77.1 us -> 83.3 us  [on_device(): lax.psum_scatter(in_part, 'tok', scatter_dimension=0, tiled=True)]
  transfers between devices with their start and end apart: 12 -> 26, of which waited for: 11 -> 23; matrix products, arithmetic and copies ran while one was open for 0% -> 3% of each run, Pallas kernels for 0% -> 0%
where the time goes in v1:
time: 545 us; the launch traced here: 544 us
  waiting for transfers between devices  231 us (42%)
  blocking collectives  194 us (36%)
  starting transfers between devices  38.6 us (7%)
  local copies, waits for them, and re-layouts  26.7 us (5%)
  matrix products  23 us (4%)
  other arithmetic  16.4 us (3%)
  between operations  13.9 us (3%)
    psum x1, blocking collectives, on_device(): out_tangent = lax.psum(out_part, 'tok').astype(jnp.bfloat16)  88.2 us
    reduce_scatter x1, waiting for transfers between devices, on_device(): lax.psum_scatter(in_part, 'tok', scatter_dimension=0, tiled=True)  83.3 us
    reduce_scatter x1, waiting for transfers between devices, on_device(): lax.psum_scatter(jnp.stack([gate_part, up_part], axis=2), 'ch', scatter_d...  60.2 us
    reduce_scatter x1, waiting for transfers between devices, on_device(): lax.psum_scatter(lax.dot_general(piece, down_weight, (((1,), (1,)), ((),...  49.8 us
    psum x1, blocking collectives, on_device(): diagonal_estimate = lax.psum(token_terms, 'tok') / total_rows  38.1 us
    all_gather x1, blocking collectives, on_device(): lax.all_gather(tokens, 'tok', axis=0, tiled=True)  24.4 us
    all_gather x1, blocking collectives, on_device(): lax.all_gather(tangent, 'tok', axis=0, tiled=True)  23.3 us
    unnamed x36, local copies, waits for them, and re-layouts  21.1 us
  transfers between devices with their start and end apart: 26, of which 23 were waited for; matrix products, arithmetic and copies ran while one was open for 3% of the time, Pallas kernels for 0%

profile of v1, /device:TPU:32, one launch (start us, length us, event | category | flops | bytes accessed | tf_op | source)
XLA Modules:
  0.0 544.1 jit_solution(18397620331970088893)
XLA Ops:
  7.3 0.8 add_convert_fusion
  8.1 6.5 %fusion.3 = pred[1024,1024]{1,0:T(32,128)(4,1)S(1)} fusion(s32[1024]{0:T(1024)S(1)} %get-tuple-element.6, s32[1024]{0:T(1024)S(1)} %get-tuple-element.7, s32[1024]{0:T(1024)S(1)} %get-tuple-element.8, s32[1024]{0:T(1024)S(1)} %get-tuple-element.9, s32[1024]{0:T(1024)S(1)} %get-tuple-element.10, s32[1024]{0:T(1024)S(1)} %get-tuple-element.11, ...), kind=kLoop, calls=%fused_computation.9 | loop fusion | flops 32505856 | bytes 1089536 | tf_op jit(solution)/shard_map/eq | solution.py:27
  14.6 1.0 copy-done.1
  15.6 1.4 fusion.14
  17.0 1.4 collective-permute-done
  18.4 0.8 add_select_fusion.6
  19.3 1.9 collective-permute-start.1
  21.2 2.5 collective-permute-done.1
  23.7 0.8 add_select_fusion.5
  24.6 3.4 collective-permute-start.2
  27.9 2.3 collective-permute-done.2
  30.3 6.1 %collective-permute-start.3 = (f32[16,1024]{1,0:T(8,128)S(1)}, f32[16,1024]{1,0:T(8,128)S(1)}, u32[]{:S(2)}, u32[]{:S(2)}) collective-permute-start(f32[16,1024]{1,0:T(8,128)S(1)} %add_select_fusion.4), channel_id=1, source_target_pairs={{0,8},{1,9},{2,10},{3,11},{4,12},{5,13},{6,14},{7,15},{8,0},{9,1},... | collective-permute-start | bytes 196616 | tf_op jit(solution)/shard_map/ppermute | solution.py:19
  36.3 24.4 %all_gather.9 = bf16[256,1024]{1,0:T(8,128)(2,1)S(1)} all-gather(bf16[16,1024]{1,0:T(8,128)(2,1)} %param.6), channel_id=1, replica_groups=mesh['tok'=16,'ch'=16] {'tok'}, dimensions={0}, use_global_device_ids=true | all-gather | bytes 557056 | tf_op jit(solution)/shard_map/all_gather | solution.py:67
  60.7 23.3 %all_gather.10 = bf16[256,1024]{1,0:T(8,128)(2,1)S(1)} all-gather(bf16[16,1024]{1,0:T(8,128)(2,1)S(1)} %multiply_convert_fusion.2), channel_id=1, replica_groups=mesh['tok'=16,'ch'=16] {'tok'}, dimensions={0}, use_global_device_ids=true | all-gather | bytes 557056 | tf_op jit(solution)/shard_map/all_gather | solution.py:68
  84.0 4.0 fusion.11
  88.0 2.1 fusion.8
  90.1 3.2 pad_maximum_fusion
  93.4 60.2 %reduce-scatter.4.cloned.1.call-done = f32[16,2,2,1664]{3,0,1,2:T(8,128)} async-done(((f32[256,2,2,1664]{3,0,1,2:T(8,128)}), f32[16,2,2,1664]{3,0,1,2:T(8,128)}) %reduce-scatter.4.cloned.1.call-update) | async-done | bytes 426000 | tf_op jit(solution)/shard_map/reduce_scatter | solution.py:73
  153.6 1.1 fusion.24
  154.8 20.4 %all_gather.11 = bf16[256,1664]{1,0:T(8,128)(2,1)S(1)} all-gather(bf16[16,1664]{1,0:T(8,128)(2,1)S(1)} %fusion.24), channel_id=1, replica_groups=mesh['tok'=16,'ch'=16] {'ch'}, dimensions={0}, use_global_device_ids=true | all-gather | bytes 905216 | tf_op jit(solution)/shard_map/all_gather | solution.py:85
  175.2 4.1 fusion.43
  179.3 88.2 %all-reduce.1 = bf16[256,1024]{1,0:T(8,128)(2,1)} all-reduce(f32[256,1024]{1,0:T(8,128)} %fusion.43), channel_id=1, replica_groups=mesh['tok'=16,'ch'=16] {'tok'}, use_global_device_ids=true, to_apply=%region_1.2 | all-reduce | flops 262144 | bytes 1572864 | tf_op jit(solution)/shard_map/psum | solution.py:89
  267.5 4.5 fusion.44
  272.3 49.8 %reduce-scatter.6.cloned.1.call-done = f32[16,1664]{1,0:T(8,128)} async-done(((f32[256,1664]{1,0:T(8,128)}), f32[16,1664]{1,0:T(8,128)}) %reduce-scatter.6.cloned.1.call-update) | async-done | bytes 106512 | tf_op jit(solution)/shard_map/reduce_scatter | solution.py:91
  322.1 1.1 fusion.28
  323.2 4.1 collective-permute-done.4
  328.0 1.7 collective-permute-start.12
  329.7 2.4 collective-permute-done.5
  332.8 1.7 collective-permute-start.13
  334.5 1.7 collective-permute-done.6
  336.8 3.1 collective-permute-start.14
  339.9 1.6 collective-permute-done.7
  342.2 3.1 collective-permute-start.15
  345.3 1.7 collective-permute-done.8
  346.9 0.9 collective-permute-done.15
  347.9 2.9 collective-permute-start.16
  350.8 1.8 collective-permute-done.9
  353.4 3.0 collective-permute-start.17
  356.4 1.7 collective-permute-done.10
  358.7 3.2 collective-permute-start.18
  361.9 1.6 collective-permute-done.11
  364.8 1.5 bitcast_dynamic-update-slice_fusion.13
  366.3 1.5 bitcast_dynamic-update-slice_fusion.12
  367.8 1.6 bitcast_dynamic-update-slice_fusion.11
  369.4 1.5 bitcast_dynamic-update-slice_fusion.10
  370.9 1.5 bitcast_dynamic-update-slice_fusion.9
  372.5 1.5 bitcast_dynamic-update-slice_fusion.8
  374.7 1.5 bitcast_dynamic-update-slice_fusion.6
  376.2 1.5 bitcast_dynamic-update-slice_fusion.5
  377.8 1.5 bitcast_dynamic-update-slice_fusion.4
  379.3 1.5 bitcast_dynamic-update-slice_fusion.3
  382.8 3.4 gather_fusion
  386.2 1.6 copy.14
  387.8 1.2 fusion.19
  389.7 2.1 convolution_add_fusion
  391.9 83.3 %reduce-scatter.8.cloned.1.call-done = f32[16,1024]{1,0:T(8,128)} async-done(((f32[256,1024]{1,0:T(8,128)}), f32[16,1024]{1,0:T(8,128)}) %reduce-scatter.8.cloned.1.call-update) | async-done | bytes 65552 | tf_op jit(solution)/shard_map/reduce_scatter | solution.py:128
  475.2 3.6 fusion
  478.8 1.2 collective-permute-done.19
  480.6 3.8 collective-permute-done.20
  484.4 2.6 collective-permute-start.21
  487.0 2.6 collective-permute-done.21
  489.7 5.0 collective-permute-start.22
  494.7 3.5 collective-permute-done.22
  498.9 38.1 %psum.15 = f32[1024]{0:T(1024)S(1)} all-reduce(f32[1024]{0:T(1024)S(1)} %get-tuple-element.2), channel_id=1, replica_groups=mesh['tok'=16,'ch'=16] {'tok'}, use_global_device_ids=true, to_apply=%region_5.6 | all-reduce | flops 1024 | bytes 8192 | tf_op jit(solution)/shard_map/psum | solution.py:134
  (67 shorter events, 11.0 us)
Async XLA Ops:
  7.2 80.9 %copy-start = (bf16[1024,1664]{1,0:T(8,128)(2,1)S(1)}, bf16[1024,1664]{1,0:T(8,128)(2,1)}, u32[]{:S(2)}) copy-start(bf16[1024,1664]{1,0:T(8,128)(2,1)} %param.9) | copy-start | bytes 10223620
  7.2 146.5 %reduce-scatter.4.cloned.1.call-start = ((), (), s32[]{:S(2)}) async-start(), calls=%async_computation.3 | async-start | bytes 7241728 | tf_op jit(solution)/shard_map/reduce_scatter | solution.py:73
  14.6 1.0 copy-start.1
  17.0 1.4 collective-permute-start
  19.3 4.5 collective-permute-start.1
  24.6 5.7 %collective-permute-start.2 = (f32[16,1024]{1,0:T(8,128)S(1)}, f32[16,1024]{1,0:T(8,128)S(1)}, u32[]{:S(2)}, u32[]{:S(2)}) collective-permute-start(f32[16,1024]{1,0:T(8,128)S(1)} %add_select_fusion.5), channel_id=1, source_target_pairs={{0,4},{1,5},{2,6},{3,7},{4,0},{5,1},{6,2},{7,3},{8,12},{9,13},{10,... | collective-permute-start | bytes 196616 | tf_op jit(solution)/shard_map/ppermute | solution.py:19
  30.3 30.4 %collective-permute-start.3 = (f32[16,1024]{1,0:T(8,128)S(1)}, f32[16,1024]{1,0:T(8,128)S(1)}, u32[]{:S(2)}, u32[]{:S(2)}) collective-permute-start(f32[16,1024]{1,0:T(8,128)S(1)} %add_select_fusion.4), channel_id=1, source_target_pairs={{0,8},{1,9},{2,10},{3,11},{4,12},{5,13},{6,14},{7,15},{8,0},{9,1},... | collective-permute-start | bytes 196616 | tf_op jit(solution)/shard_map/ppermute | solution.py:19
  93.4 228.7 %reduce-scatter.6.cloned.1.call-start = ((), (), s32[]{:S(2)}) async-start(), calls=%async_computation.4 | async-start | bytes 1810432 | tf_op jit(solution)/shard_map/reduce_scatter | solution.py:91
  272.1 203.1 %reduce-scatter.8.cloned.1.call-start = ((), (), s32[]{:S(2)}) async-start(), calls=%async_computation.5 | async-start | bytes 1114112 | tf_op jit(solution)/shard_map/reduce_scatter | solution.py:128
  323.2 4.1 collective-permute-start.4
  327.3 0.6 copy-start.2
  328.0 4.1 collective-permute-start.5
  328.0 4.1 collective-permute-start.12
  332.1 4.7 copy-start.4
  332.1 4.1 collective-permute-start.6
  332.1 0.7 copy-start.3
  332.8 4.0 collective-permute-start.13
  336.2 5.9 %copy-start.6 = (bf16[16,2,1664]{2,0,1:T(8,128)(2,1)}, bf16[16,2,1664]{2,0,1:T(8,128)(2,1)S(1)}, u32[]{:S(2)}) copy-start(bf16[16,2,1664]{2,0,1:T(8,128)(2,1)S(1)} %collective-permute-done.6) | copy-start | bytes 319492
  336.2 5.2 collective-permute-start.7
  336.8 3.1 copy-start.5
  336.8 5.4 collective-permute-start.14
  341.5 3.8 copy-start.7
  341.5 5.4 %collective-permute-start.8 = (bf16[16,2,1664]{2,0,1:T(8,128)(2,1)S(1)}, bf16[16,2,1664]{2,0,1:T(8,128)(2,1)}, u32[]{:S(2)}, u32[]{:S(2)}) collective-permute-start(bf16[16,2,1664]{2,0,1:T(8,128)(2,1)S(1)} %collective-permute-done.7), channel_id=1, source_target_pairs={{0,1},{1,2},{2,3},{3,4},{4,5},{5,6},{6,7},{7,8},{8,9},{9,10},{10,1... | collective-permute-start | bytes 319496 | tf_op jit(solution)/shard_map/ppermute | solution.py:115
  342.2 5.7 %collective-permute-start.15 = (bf16[16,2,1664]{2,0,1:T(8,128)(2,1)}, bf16[16,2,1664]{2,0,1:T(8,128)(2,1)}, u32[]{:S(2)}, u32[]{:S(2)}) collective-permute-start(bf16[16,2,1664]{2,0,1:T(8,128)(2,1)} %collective-permute-done.14), channel_id=1, source_target_pairs={{1,0},{2,1},{3,2},{4,3},{5,4},{6,5},{7,6},{8,7},{9,8},{10,9},{11,1... | collective-permute-start | bytes 319496 | tf_op jit(solution)/shard_map/ppermute | solution.py:118
  346.9 5.7 %collective-permute-start.9 = (bf16[16,2,1664]{2,0,1:T(8,128)(2,1)}, bf16[16,2,1664]{2,0,1:T(8,128)(2,1)}, u32[]{:S(2)}, u32[]{:S(2)}) collective-permute-start(bf16[16,2,1664]{2,0,1:T(8,128)(2,1)} %collective-permute-done.8), channel_id=1, source_target_pairs={{0,1},{1,2},{2,3},{3,4},{4,5},{5,6},{6,7},{7,8},{8,9},{9,10},{10,1... | collective-permute-start | bytes 319496 | tf_op jit(solution)/shard_map/ppermute | solution.py:115
  347.9 5.6 %collective-permute-start.16 = (bf16[16,2,1664]{2,0,1:T(8,128)(2,1)}, bf16[16,2,1664]{2,0,1:T(8,128)(2,1)S(1)}, u32[]{:S(2)}, u32[]{:S(2)}) collective-permute-start(bf16[16,2,1664]{2,0,1:T(8,128)(2,1)} %collective-permute-done.15), channel_id=1, source_target_pairs={{1,0},{2,1},{3,2},{4,3},{5,4},{6,5},{7,6},{8,7},{9,8},{10,9},{11,1... | collective-permute-start | bytes 319496 | tf_op jit(solution)/shard_map/ppermute | solution.py:118
  352.6 5.6 %collective-permute-start.10 = (bf16[16,2,1664]{2,0,1:T(8,128)(2,1)}, bf16[16,2,1664]{2,0,1:T(8,128)(2,1)S(1)}, u32[]{:S(2)}, u32[]{:S(2)}) collective-permute-start(bf16[16,2,1664]{2,0,1:T(8,128)(2,1)} %collective-permute-done.9), channel_id=1, source_target_pairs={{0,1},{1,2},{2,3},{3,4},{4,5},{5,6},{6,7},{7,8},{8,9},{9,10},{10,1... | collective-permute-start | bytes 319496 | tf_op jit(solution)/shard_map/ppermute | solution.py:115
  353.4 5.3 collective-permute-start.17
  358.1 5.3 collective-permute-start.11
  358.7 23.4 %collective-permute-start.18 = (bf16[16,2,1664]{2,0,1:T(8,128)(2,1)S(1)}, bf16[16,2,1664]{2,0,1:T(8,128)(2,1)S(1)}, u32[]{:S(2)}, u32[]{:S(2)}) collective-permute-start(bf16[16,2,1664]{2,0,1:T(8,128)(2,1)S(1)} %collective-permute-done.17), channel_id=1, source_target_pairs={{1,0},{2,1},{3,2},{4,3},{5,4},{6,5},{7,6},{8,7},{9,8},{10,9},{11,1... | collective-permute-start | bytes 319496 | tf_op jit(solution)/shard_map/ppermute | solution.py:118
  387.8 2.0 copy-start.10
  391.9 102.8 %copy-start.9 = (s32[1024]{0:T(1024)S(1)}, s32[1024]{0:T(1024)}, u32[]{:S(2)}) copy-start(s32[1024]{0:T(1024)} %param.8) | copy-start | bytes 12292
  391.9 106.3 %copy-start.8 = (s32[16,1024]{1,0:T(8,128)S(1)}, s32[16,1024]{1,0:T(8,128)}, u32[]{:S(2)}) copy-start(s32[16,1024]{1,0:T(8,128)} %param.7) | copy-start | bytes 196612
  478.8 1.3 collective-permute-start.19
  480.0 4.4 collective-permute-start.20
  484.4 5.3 collective-permute-start.21
  489.7 8.5 %collective-permute-start.22 = (f32[16,1024]{1,0:T(8,128)S(1)}, f32[16,1024]{1,0:T(8,128)S(1)}, u32[]{:S(2)}, u32[]{:S(2)}) collective-permute-start(f32[16,1024]{1,0:T(8,128)S(1)} %add_select_fusion.1), channel_id=1, source_target_pairs={{0,8},{1,9},{2,10},{3,11},{4,12},{5,13},{6,14},{7,15},{8,0},{9,1},... | collective-permute-start | bytes 196616 | tf_op jit(solution)/shard_map/ppermute | solution.py:19
Sparse Core Ops, SparseCore 0:
  93.5 60.0 reduce-scatter.3
  272.2 49.8 reduce-scatter.5
  392.0 83.1 reduce-scatter.7
